TPU v7x, 512 devices: a whole 4x4x16 slice. The times are simulated.
512 devices in a mesh: wide: 64 (over x, y, z_hi), grp: 8 (over z_lo, core).
Axes of the slice: x: 4, y: 4, z: 16 (z_hi: 4, z_lo: 4; z = z_hi * 4 + z_lo), core: 2. Of those that a mesh axis runs over, the one named last changes fastest.
Arguments:
- samples: bfloat16 [2048, 512], P(('wide', 'grp')), may hold values from -6 to 6
- archive: bfloat16 [262144, 512], P(('wide', 'grp')), may hold values from -6 to 6
- inv_len: float32 [512], replicated, may hold values from 0.7 to 2.8
- mean_coef: bfloat16 [262144, 64], P(('wide', 'grp')), may hold values from -0.1875 to 0.1875
- var_coef: bfloat16 [262144, 64], P(('wide', 'grp')), may hold values from -1 to 1
Outputs:
- pred_mean: float32 [2048, 64], P(('wide', 'grp'))
- pred_var: float32 [2048, 64], P(('wide', 'grp'))
All inputs are finite; a program needn't handle non-finite values.
Results may differ from a plain program's by a relative error of at most 0.0085.
Values may be sent and summed in bfloat16 or wider, within the bound.
A program may use at most 64 MiB of HBM per device.

v0:
```python
import jax
import jax.numpy as jnp
from jax import lax
from jax.sharding import PartitionSpec as P

DIN = 512


def scaled_rows(rows, inv_len):
    factor = inv_len * DIN ** (-0.5)
    scaled = (rows.astype(jnp.float32) * factor).astype(jnp.bfloat16)
    wide_copy = scaled.astype(jnp.float32)
    return (scaled, jnp.sum(wide_copy * wide_copy, axis=-1))


def on_device(samples, archive, inv_len, mean_coef, var_coef):
    gathered = lax.all_gather(samples, ("wide", "grp"), axis=0, tiled=True)
    samp_z, samp_norm = scaled_rows(gathered, inv_len)
    arch_z, arch_norm = scaled_rows(archive, inv_len)
    local_runs = archive.shape[0]
    block_rows = min(128, local_runs)
    block_count = local_runs // block_rows
    width = mean_coef.shape[1]
    arch_blocks = arch_z.reshape(block_count, block_rows, DIN)
    norm_blocks = arch_norm.reshape(block_count, block_rows)
    mean_blocks = mean_coef.reshape(block_count, block_rows, width)
    var_blocks = var_coef.reshape(block_count, block_rows, width)
    own_rows = samples.shape[0]

    def accumulate(totals, pieces):
        mean_sum, corr_sum = totals
        block_z, block_norm, mean_rows, var_rows = pieces
        inner_prod = lax.dot_general(
            samp_z, block_z, (((1,), (1,)), ((), ())), preferred_element_type=jnp.float32
        )
        kernel = jnp.exp(inner_prod - 0.5 * samp_norm[:, None] - 0.5 * block_norm[None, :])
        kernel_half = kernel.astype(jnp.bfloat16)
        square_half = (kernel * kernel).astype(jnp.bfloat16)
        mean_sum = mean_sum + jnp.dot(kernel_half, mean_rows, preferred_element_type=jnp.float32)
        corr_sum = corr_sum + jnp.dot(square_half, var_rows, preferred_element_type=jnp.float32)
        return ((mean_sum, corr_sum), None)

    start_pair = (
        jnp.zeros((own_rows * lax.axis_size(("wide", "grp")), width), jnp.float32),
        jnp.zeros((own_rows * lax.axis_size(("wide", "grp")), width), jnp.float32),
    )
    final_pair, unused = lax.scan(
        accumulate, start_pair, (arch_blocks, norm_blocks, mean_blocks, var_blocks)
    )
    summed = lax.psum_scatter(
        jnp.concatenate([final_pair[0], final_pair[1]], axis=1),
        ("wide", "grp"),
        scatter_dimension=0,
        tiled=True,
    )
    pred_mean = summed[:, :width]
    pred_var = 1.0 - summed[:, width:]
    return (pred_mean, pred_var)


def solution(mesh):
    in_specs = (
        P(("wide", "grp"), None),
        P(("wide", "grp"), None),
        P(),
        P(("wide", "grp"), None),
        P(("wide", "grp"), None),
    )
    out_specs = (P(("wide", "grp"), None), P(("wide", "grp"), None))
    return jax.shard_map(
        on_device, mesh=mesh, in_specs=in_specs, out_specs=out_specs, check_vma=False
    )
```

profile of v0, /device:TPU:1, one launch (start us, length us, event | category | flops | bytes accessed | tf_op | source)
XLA Modules:
  0.0 715.8 jit_solution(6088330128535756338)
XLA Ops:
  7.2 0.0 all-gather.3.cloned.1.call-start
  7.2 0.7 all-gather.3.cloned.1.call-update
  7.9 0.0 all-reduce.3.cloned.1.call-start
  8.0 1.0 copy.11
  8.9 1.0 copy.12
  9.9 0.7 broadcast_multiply_fusion.1
  10.6 2.0 multiply_reduce_fusion.1
  12.6 199.4 %all-gather.3.cloned.1.call-done = bf16[512,4,512]{2,1,0:T(4,128)(2,1)} async-done(((bf16[1,4,512]{2,1,0:T(4,128)(2,1)}), bf16[512,4,512]{2,1,0:T(4,128)(2,1)}) %all-gather.3.cloned.1.call-update) | async-done | bytes 2097168 | tf_op jit(solution)/shard_map/all_gather | solution.py:17
  212.0 4.2 reshape.27
  216.2 2.8 multiply_reduce_fusion
  218.9 21.9 %while.13 = (s32[]{:T(128)}, f32[2048,64]{0,1:T(8,128)}, f32[2048,64]{0,1:T(8,128)}, bf16[4,128,512]{2,1,0:T(8,128)(2,1)}, bf16[2048,512]{1,0:T(8,128)(2,1)S(1)}...) while((s32[]{:T(128)}, f32[2048,64]{0,1:T(8,128)}, ...), condition=%wide.region_3.4_spmd.clone, body=%wide.region_2.3_spmd.clone.sunk | while | flops 337381504 | bytes 7563396 | solution.py:47
  219.0 1.7 fusion.28
  220.7 1.1 convolution_add_fusion.5
  221.8 1.1 convolution_add_fusion.4
  222.9 1.7 fusion.28
  224.6 2.1 convolution_add_fusion.5
  226.7 2.1 convolution_add_fusion.4
  228.9 1.7 fusion.28
  230.6 2.1 convolution_add_fusion.5
  232.7 2.1 convolution_add_fusion.4
  234.9 1.7 fusion.28
  236.6 2.1 convolution_add_fusion.5
  238.7 2.1 convolution_add_fusion.4
  240.8 1.4 copy.13
  242.2 1.4 copy.14
  243.6 1.4 pad_maximum_fusion
  245.0 0.0 all-reduce.3.cloned.1.call-update
  245.0 462.6 %all-reduce.3.cloned.1.call-done = f32[2048,128]{1,0:T(8,128)} async-done(((f32[2048,128]{1,0:T(8,128)}), f32[2048,128]{1,0:T(8,128)}) %all-reduce.3.cloned.1.call-update) | async-done | bytes 1048592
  707.6 0.7 constant_dynamic-slice_fusion.1
  708.3 0.7 slice_subtract_fusion
  (10 shorter events, 0.0 us)
Async XLA Ops:
  7.2 204.8 %all-gather.3.cloned.1.call-start = ((), (), s32[]{:S(2)}) async-start(), calls=%async_computation | async-start | bytes 2101248 | tf_op jit(solution)/shard_map/all_gather | solution.py:17
  7.9 699.7 %all-reduce.3.cloned.1.call-start = ((), (), s32[]{:S(2)}) async-start(), calls=%async_computation.1 | async-start | bytes 2097152
Sparse Core Ops, SparseCore 0:
  12.6 199.3 all-gather.2
  245.1 462.4 all-reduce.2
where the time goes:
time: 717 us; the launch traced here: 716 us
  waiting for transfers between devices  663 us (92%)
  matrix products  21.8 us (3%)
  between operations  14.1 us (2%)
  local copies, waits for them, and re-layouts  9.55 us (1%)
  other arithmetic  7.5 us (1%)
    unnamed x3, waiting for transfers between devices  463 us
    all_gather x1, waiting for transfers between devices, on_device(): gathered = lax.all_gather(samples, ('wide', 'grp'), axis=0, tiled=True)  199 us
  transfers between devices with their start and end apart: 2, of which 2 were waited for; matrix products, arithmetic and copies ran while one was open for 1% of the time, Pallas kernels for 0%

commit v1 on v0

--- a/solution.py
+++ b/solution.py
@@ -14,7 +14,12 @@
 
 
 def on_device(samples, archive, inv_len, mean_coef, var_coef):
-    gathered = lax.all_gather(samples, ("wide", "grp"), axis=0, tiled=True)
+    gathered = jnp.concatenate(
+        lax.all_to_all(
+            jnp.stack([samples] * lax.axis_size(("wide", "grp"))), ("wide", "grp"), 0, 0
+        ),
+        axis=0,
+    )
     samp_z, samp_norm = scaled_rows(gathered, inv_len)
     arch_z, arch_norm = scaled_rows(archive, inv_len)
     local_runs = archive.shape[0]

time: 717 us -> 623 us (0.87)
  waiting for transfers between devices: 663 us -> 556 us
  starting transfers between devices: 0.08 us -> 24.3 us
  matrix products: 21.8 us -> 12.4 us
    all_gather x1 -> x0, waiting for transfers between devices: 199 us -> none  [on_device(): gathered = lax.all_gather(samples, ('wide', 'grp'), axis=0, tiled=True)]
    all_to_all x0 -> x1, waiting for transfers between devices: none -> 97.9 us  [on_device(): lax.all_to_all(jnp.stack([samples] * lax.axis_size(('wide', 'grp'))), ('w...]
    all_to_all x0 -> x1, starting transfers between devices: none -> 24.3 us  [on_device(): lax.all_to_all(jnp.stack([samples] * lax.axis_size(('wide', 'grp'))), ('w...]
    unnamed x3 -> x2, waiting for transfers between devices: 463 us -> 458 us
  transfers between devices with their start and end apart: 2 -> 2, of which waited for: 2 -> 2; matrix products, arithmetic and copies ran while one was open for 1% -> 0% of each run, Pallas kernels for 0% -> 0%
where the time goes in v1:
time: 623 us
  waiting for transfers between devices  556 us (89%)
  starting transfers between devices  24.3 us (4%)
  between operations  14.1 us (2%)
  matrix products  12.4 us (2%)
  other arithmetic  8.25 us (1%)
  local copies, waits for them, and re-layouts  7.48 us (1%)
    unnamed x2, waiting for transfers between devices  458 us
    all_to_all x1, waiting for transfers between devices, on_device(): lax.all_to_all(jnp.stack([samples] * lax.axis_size(('wide', 'grp'))), ('w...  97.9 us
    all_to_all x1, starting transfers between devices, on_device(): lax.all_to_all(jnp.stack([samples] * lax.axis_size(('wide', 'grp'))), ('w...  24.3 us
  transfers between devices with their start and end apart: 2, of which 2 were waited for; matrix products, arithmetic and copies ran while one was open for 0% of the time, Pallas kernels for 0%

profile of v1, /device:TPU:1, one launch (start us, length us, event | category | flops | bytes accessed | tf_op | source)
XLA Modules:
  0.0 622.7 jit_solution(14583770266473302559)
XLA Ops:
  7.2 0.0 copy-start
  7.2 2.6 stack.2
  9.8 24.3 %all-to-all-start = ((bf16[512,4,512]{2,1,0:T(4,128)(2,1)}), bf16[512,4,512]{2,1,0:T(4,128)(2,1)S(1)}, u32[]{:S(2)}, u32[]{:S(2)}) async-start(bf16[512,4,512]{2,1,0:T(4,128)(2,1)} %stack.2), calls=%async_computation | async-start | bytes 4194304 | tf_op jit(solution)/shard_map/all_to_all | solution.py:18
  34.1 0.0 all-reduce.3.cloned.1.call-start
  34.2 0.1 copy.15
  34.3 0.8 copy.16
  35.1 2.0 multiply_reduce_fusion.1
  37.1 97.9 %all-to-all-done = bf16[512,4,512]{2,1,0:T(4,128)(2,1)S(1)} async-done(((bf16[512,4,512]{2,1,0:T(4,128)(2,1)}), bf16[512,4,512]{2,1,0:T(4,128)(2,1)S(1)}, u32[]{:S(2)}, u32[]{:S(2)}) %all-to-all-start) | async-done | bytes 2097184 | tf_op jit(solution)/shard_map/all_to_all | solution.py:18
  135.0 1.4 multiply_reduce_fusion
  136.4 0.2 reduce_sum.21
  136.6 2.5 reshape.35
  139.1 2.8 multiply_convert_fusion.3
  141.8 12.7 %while.13 = (s32[]{:T(128)}, f32[2048,64]{0,1:T(8,128)S(1)}, f32[2048,64]{0,1:T(8,128)S(1)}, bf16[4,128,512]{2,1,0:T(8,128)(2,1)}, bf16[2048,512]{1,0:T(8,128)(2...) while((s32[]{:T(128)}, f32[2048,64]{0,1:T(8,128)S(1)}, ...), condition=%wide.region_3.4_spmd.clone, body=%wide.region_2.3_spmd.clone.sunk | while | flops 337381504 | bytes 7562896 | solution.py:52
  141.9 1.7 fusion.28
  143.6 1.1 convolution_add_fusion.5
  144.7 0.3 convolution_add_fusion.4
  145.0 1.7 fusion.28
  146.8 1.1 convolution_add_fusion.5
  147.8 0.3 convolution_add_fusion.4
  148.2 1.7 fusion.28
  149.9 1.1 convolution_add_fusion.5
  151.0 0.3 convolution_add_fusion.4
  151.4 1.7 fusion.28
  153.1 1.1 convolution_add_fusion.5
  154.2 0.3 convolution_add_fusion.4
  154.5 0.3 copy.18
  154.8 0.3 copy.17
  155.2 1.4 pad_maximum_fusion
  156.5 0.0 all-reduce.3.cloned.1.call-update
  156.6 457.9 %all-reduce.3.cloned.1.call-done = f32[2048,128]{1,0:T(8,128)} async-done(((f32[2048,128]{1,0:T(8,128)}), f32[2048,128]{1,0:T(8,128)}) %all-reduce.3.cloned.1.call-update) | async-done | bytes 1048592
  614.5 0.7 constant_dynamic-slice_fusion.1
  615.2 0.7 slice_subtract_fusion
  (16 shorter events, 0.1 us)
Async XLA Ops:
  7.2 27.0 %copy-start = (bf16[512,64]{0,1:T(8,128)(2,1)S(1)}, bf16[512,64]{0,1:T(8,128)(2,1)}, u32[]{:S(2)}) copy-start(bf16[512,64]{0,1:T(8,128)(2,1)} %param.10) | copy-start | bytes 196612
  7.2 27.1 %copy-start.1 = (bf16[512,64]{0,1:T(8,128)(2,1)S(1)}, bf16[512,64]{0,1:T(8,128)(2,1)}, u32[]{:S(2)}) copy-start(bf16[512,64]{0,1:T(8,128)(2,1)} %param.11) | copy-start | bytes 196612
  7.2 27.9 %copy-start.2 = (f32[512]{0:T(512)S(1)}, f32[512]{0:T(512)}, u32[]{:S(2)}) copy-start(f32[512]{0:T(512)} %param.9) | copy-start | bytes 6148
  9.8 125.2 %all-to-all-start = ((bf16[512,4,512]{2,1,0:T(4,128)(2,1)}), bf16[512,4,512]{2,1,0:T(4,128)(2,1)S(1)}, u32[]{:S(2)}, u32[]{:S(2)}) async-start(bf16[512,4,512]{2,1,0:T(4,128)(2,1)} %stack.2), calls=%async_computation | async-start | bytes 4194304 | tf_op jit(solution)/shard_map/all_to_all | solution.py:18
  34.1 580.4 %all-reduce.3.cloned.1.call-start = ((), (), s32[]{:S(2)}) async-start(), calls=%async_computation.1 | async-start | bytes 2097152
Sparse Core Ops, SparseCore 0:
  156.7 457.7 all-reduce.2
